TPU v7x, 512 devices: a whole 4x8x8 slice. The times are simulated.
512 devices in a mesh: row: 32 (over z, y_hi, core), col: 16 (over x, y_lo).
Axes of the slice: x: 4, y: 8 (y_hi: 2, y_lo: 4; y = y_hi * 4 + y_lo), z: 8, core: 2. Of those that a mesh axis runs over, the one named last changes fastest.
Arguments:
- rhs_top: bfloat16 [2, 1024, 16384], P(None, 'row', 'col'), may hold values from -6 to 6
- diag_inverse: bfloat16 [2, 1024, 1024], P(None, 'row'), as said below
- panel_coupling: bfloat16 [1024, 1024], P('row'), may hold values from -0.1875 to 0.1875
- trailing_factor: bfloat16 [32768, 2048], P('row', 'col'), may hold values from -0.125 to 0.125
- rhs_trailing: bfloat16 [32768, 16384], P('row', 'col'), may hold values from -6 to 6
Outputs:
- solved: bfloat16 [2, 1024, 16384], P(None, 'row', 'col')
- updated: bfloat16 [32768, 16384], P('row', 'col')
Inputs may be any that keep to these rules, and one draw needn't show every extreme that they name: Each diag_inverse[k] is lower triangular.
All inputs are finite; a program needn't handle non-finite values.
Results may differ from a plain program's by a relative error of at most 0.0055.
Values may be sent and summed in bfloat16 or wider, within the bound.
A program may use at most 64 MiB of HBM per device.

v0:
```python
import jax
import jax.numpy as jnp
from jax import lax
from jax.sharding import PartitionSpec as P


def fold_rows(inverse_rows, piece):
    return jnp.dot(inverse_rows, piece, preferred_element_type=jnp.float32)


def shards(rhs_top, diag_inverse, panel_coupling, trailing_factor, rhs_trailing):
    inverse_first = diag_inverse[0]
    inverse_second = diag_inverse[1]
    first_mine = fold_rows(
        inverse_first, lax.all_gather(rhs_top[0], "row", axis=0, tiled=True)
    ).astype(jnp.bfloat16)
    first_all = lax.all_gather(first_mine, "row", axis=0, tiled=True)
    carried = (
        rhs_top[1].astype(jnp.float32)
        - jnp.dot(panel_coupling, first_all, preferred_element_type=jnp.float32)
    ).astype(jnp.bfloat16)
    second_mine = fold_rows(
        inverse_second, lax.all_gather(carried, "row", axis=0, tiled=True)
    ).astype(jnp.bfloat16)
    second_all = lax.all_gather(second_mine, "row", axis=0, tiled=True)
    solution = jnp.concatenate([first_all, second_all], axis=0)
    total = jnp.dot(
        lax.all_gather(trailing_factor, "col", axis=1, tiled=True),
        solution,
        preferred_element_type=jnp.float32,
    )
    updated = (rhs_trailing.astype(jnp.float32) - total).astype(jnp.bfloat16)
    solved = jnp.stack([first_mine, second_mine])
    return (solved, updated)


def solution(mesh):
    in_specs = (
        P(None, "row", "col"),
        P(None, "row", None),
        P("row", None),
        P("row", "col"),
        P("row", "col"),
    )
    out_specs = (P(None, "row", "col"), P("row", "col"))
    return jax.shard_map(shards, mesh=mesh, in_specs=in_specs, out_specs=out_specs, check_vma=False)
```

profile of v0, /device:TPU:9, one launch (start us, length us, event | category | flops | bytes accessed | tf_op | source)
XLA Modules:
  0.0 514.1 jit_solution(12273619999213910419)
XLA Ops:
  7.2 0.0 copy-start
  7.2 0.0 copy-start.5
  7.2 0.0 all-gather.15.cloned.1.call-start
  7.2 1.5 slice.13
  8.7 0.0 all-gather.15.cloned.1.call-update
  8.8 0.0 copy-start.4
  8.8 0.0 all-gather.7.cloned.1.call-start
  8.8 101.2 %all-gather.15.cloned.1.call-done = bf16[1,1024,1024]{2,1,0:T(8,128)(2,1)} async-done(((bf16[1,32,1024]{2,1,0:T(8,128)(2,1)}), bf16[1,1024,1024]{2,1,0:T(8,128)(2,1)}) %all-gather.15.cloned.1.call-update) | async-done | bytes 2097168 | tf_op jit(solution)/shard_map/all_gather | solution.py:15
  110.0 2.7 fusion.11
  112.7 0.0 all-gather.7.cloned.1.call-update
  112.8 0.0 copy-start.1
  112.8 0.0 all-gather.9.cloned.1.call-start
  112.8 88.3 %all-gather.7.cloned.1.call-done = bf16[1024,1024]{1,0:T(8,128)(2,1)} async-done(((bf16[32,1024]{1,0:T(8,128)(2,1)}), bf16[1024,1024]{1,0:T(8,128)(2,1)}) %all-gather.7.cloned.1.call-update) | async-done | bytes 2097168 | tf_op jit(solution)/shard_map/all_gather | solution.py:17
  201.2 0.0 copy-done
  201.2 0.0 copy-done.5
  201.2 2.7 fusion.10
  203.9 0.0 all-gather.9.cloned.1.call-update
  203.9 0.0 all-gather.13.cloned.1.call-start
  203.9 0.5 all-gather.13.cloned.1.call-update
  204.5 0.0 all-gather.11.cloned.1.call-start
  204.5 87.8 %all-gather.9.cloned.1.call-done = bf16[1024,1024]{1,0:T(8,128)(2,1)} async-done(((bf16[32,1024]{1,0:T(8,128)(2,1)}), bf16[1024,1024]{1,0:T(8,128)(2,1)}) %all-gather.9.cloned.1.call-update) | async-done | bytes 2097168 | tf_op jit(solution)/shard_map/all_gather | solution.py:23
  292.3 0.0 copy-done.4
  292.3 2.7 convolution_convert_fusion
  295.0 0.0 all-gather.11.cloned.1.call-update
  295.0 0.0 copy-done.1
  295.0 0.0 copy-start.2
  295.1 0.0 copy-start.3
  295.1 2.6 copy.7
  297.6 0.0 copy-done.2
  297.6 0.0 copy-done.3
  297.6 0.7 pad_maximum_fusion
  298.3 98.5 %all-gather.13.cloned.1.call-done = bf16[1024,2048]{1,0:T(8,128)(2,1)} async-done(((bf16[1024,128]{1,0:T(8,128)(2,1)}), bf16[1024,2048]{1,0:T(8,128)(2,1)}) %all-gather.13.cloned.1.call-update) | async-done | bytes 4194320 | tf_op jit(solution)/shard_map/all_gather | solution.py:28
  396.8 99.6 %all-gather.11.cloned.1.call-done = bf16[1024,1024]{1,0:T(8,128)(2,1)} async-done(((bf16[32,1024]{1,0:T(8,128)(2,1)}), bf16[1024,1024]{1,0:T(8,128)(2,1)}) %all-gather.11.cloned.1.call-update) | async-done | bytes 2097168 | tf_op jit(solution)/shard_map/all_gather | solution.py:25
  496.4 8.6 %fusion.4 = bf16[1024,1024]{0,1:T(8,128)(2,1)S(1)} fusion(bf16[1024,1024]{0,1:T(8,128)(2,1)} %copy.7, bf16[1024,2048]{1,0:T(8,128)(2,1)} %all-gather.13.cloned.1.call-done, bf16[1024,1024]{1,0:T(8,128)(2,1)} %all-gather.11.cloned.1.call-done, bf16[1024,1024]{1,0:T(8,128)(2,1)} %all-gather.7.cloned.1.call-done), kind=kOutput, calls=%fused_computation.5 | convolution fusion | flops 4306501632 | bytes 12582912 | tf_op jit(solution)/shard_map/dot_general | solution.py:27
  505.0 2.6 copy.8
Async XLA Ops:
  7.2 194.0 %copy-start = (bf16[32,1024]{1,0:T(8,128)(2,1)S(1)}, bf16[32,1024]{1,0:T(8,128)(2,1)}, u32[]{:S(2)}) copy-start(bf16[32,1024]{1,0:T(8,128)(2,1)} %param.7) | copy-start | bytes 196612
  7.2 194.0 %copy-start.5 = (bf16[2,32,1024]{2,1,0:T(8,128)(2,1)S(1)}, bf16[2,32,1024]{2,1,0:T(8,128)(2,1)}, u32[]{:S(2)}) copy-start(bf16[2,32,1024]{2,1,0:T(8,128)(2,1)} %param.5) | copy-start | bytes 393220
  7.2 102.8 %all-gather.15.cloned.1.call-start = ((), (), s32[]{:S(2)}) async-start(), calls=%async_computation.4 | async-start | bytes 2162688 | tf_op jit(solution)/shard_map/all_gather | solution.py:15
  8.8 283.6 %copy-start.4 = (bf16[2,32,1024]{2,1,0:T(8,128)(2,1)S(1)}, bf16[2,32,1024]{2,1,0:T(8,128)(2,1)}, u32[]{:S(2)}) copy-start(bf16[2,32,1024]{2,1,0:T(8,128)(2,1)} %param.6) | copy-start | bytes 393220
  8.8 192.4 %all-gather.7.cloned.1.call-start = ((), (), s32[]{:S(2)}) async-start(), calls=%async_computation | async-start | bytes 2162688 | tf_op jit(solution)/shard_map/all_gather | solution.py:17
  112.8 182.3 %copy-start.1 = (bf16[1024,1024]{1,0:T(8,128)(2,1)S(1)}, bf16[1024,1024]{1,0:T(8,128)(2,1)}, u32[]{:S(2)}) copy-start(bf16[1024,1024]{1,0:T(8,128)(2,1)} %param.9) | copy-start | bytes 6291460
  112.8 179.5 %all-gather.9.cloned.1.call-start = ((), (), s32[]{:S(2)}) async-start(), calls=%async_computation.1 | async-start | bytes 2162688 | tf_op jit(solution)/shard_map/all_gather | solution.py:23
  203.9 192.9 %all-gather.13.cloned.1.call-start = ((), (), s32[]{:S(2)}) async-start(), calls=%async_computation.3 | async-start | bytes 4456448 | tf_op jit(solution)/shard_map/all_gather | solution.py:28
  204.5 292.0 %all-gather.11.cloned.1.call-start = ((), (), s32[]{:S(2)}) async-start(), calls=%async_computation.2 | async-start | bytes 2162688 | tf_op jit(solution)/shard_map/all_gather | solution.py:25
  295.0 2.6 copy-start.2
  295.1 2.6 copy-start.3
Sparse Core Ops, SparseCore 0:
  12.0 97.9 all-gather.14
  114.0 87.1 all-gather.6
  205.1 87.1 all-gather.8
  294.2 102.5 all-gather.12
  400.0 96.3 all-gather.10
where the time goes:
time: 514 us
  waiting for transfers between devices  476 us (93%)
  matrix products  16.7 us (3%)
  between operations  13.8 us (3%)
  local copies, waits for them, and re-layouts  6.67 us (1%)
    all_gather x1, waiting for transfers between devices, shards(): lax.all_gather(rhs_top[0], 'row', axis=0, tiled=True)  101 us
    all_gather x1, waiting for transfers between devices, shards(): second_all = lax.all_gather(second_mine, 'row', axis=0, tiled=True)  99.6 us
    all_gather x1, waiting for transfers between devices, shards(): lax.all_gather(trailing_factor, 'col', axis=1, tiled=True)  98.5 us
    all_gather x1, waiting for transfers between devices, shards(): first_all = lax.all_gather(first_mine, 'row', axis=0, tiled=True)  88.3 us
    all_gather x1, waiting for transfers between devices, shards(): lax.all_gather(carried, 'row', axis=0, tiled=True)  87.8 us
  transfers between devices with their start and end apart: 5, of which 5 were waited for; matrix products, arithmetic and copies ran while one was open for 1% of the time, Pallas kernels for 0%

commit v1 on v0

--- a/solution.py
+++ b/solution.py
@@ -14,7 +14,9 @@
     first_mine = fold_rows(
         inverse_first, lax.all_gather(rhs_top[0], "row", axis=0, tiled=True)
     ).astype(jnp.bfloat16)
-    first_all = lax.all_gather(first_mine, "row", axis=0, tiled=True)
+    first_all = jnp.concatenate(
+        lax.all_to_all(jnp.stack([first_mine] * lax.axis_size("row")), "row", 0, 0), axis=0
+    )
     carried = (
         rhs_top[1].astype(jnp.float32)
         - jnp.dot(panel_coupling, first_all, preferred_element_type=jnp.float32)

time: 514 us -> 488 us (0.949)
  waiting for transfers between devices: 476 us -> 388 us
  blocking collectives: 0 us -> 59.8 us
    all_gather x1 -> x0, waiting for transfers between devices: 88.3 us -> none  [shards(): first_all = lax.all_gather(first_mine, 'row', axis=0, tiled=True)]
    all_to_all x0 -> x1, blocking collectives: none -> 59.8 us  [shards(): lax.all_to_all(jnp.stack([first_mine] * lax.axis_size('row')), 'row', 0, 0)]
  transfers between devices with their start and end apart: 5 -> 4, of which waited for: 5 -> 4; matrix products, arithmetic and copies ran while one was open for 1% -> 2% of each run, Pallas kernels for 0% -> 0%
where the time goes in v1:
time: 488 us; the launch traced here: 487 us
  waiting for transfers between devices  388 us (80%)
  blocking collectives  59.8 us (12%)
  matrix products  15.2 us (3%)
  between operations  13.8 us (3%)
  local copies, waits for them, and re-layouts  9.66 us (2%)
    all_gather x1, waiting for transfers between devices, shards(): lax.all_gather(rhs_top[0], 'row', axis=0, tiled=True)  101 us
    all_gather x1, waiting for transfers between devices, shards(): second_all = lax.all_gather(second_mine, 'row', axis=0, tiled=True)  99.6 us
    all_gather x1, waiting for transfers between devices, shards(): lax.all_gather(trailing_factor, 'col', axis=1, tiled=True)  97.3 us
    all_gather x1, waiting for transfers between devices, shards(): lax.all_gather(carried, 'row', axis=0, tiled=True)  89.1 us
    all_to_all x1, blocking collectives, shards(): lax.all_to_all(jnp.stack([first_mine] * lax.axis_size('row')), 'row', 0, 0)  59.8 us
  transfers between devices with their start and end apart: 4, of which 4 were waited for; matrix products, arithmetic and copies ran while one was open for 2% of the time, Pallas kernels for 0%

profile of v1, /device:TPU:9, one launch (start us, length us, event | category | flops | bytes accessed | tf_op | source)
XLA Modules:
  0.0 487.2 jit_solution(7353547653526887593)
XLA Ops:
  7.2 0.0 copy-start
  7.2 0.0 all-gather.12.cloned.1.call-start
  7.2 1.5 slice.13
  8.7 0.0 all-gather.12.cloned.1.call-update
  8.7 0.0 all-gather.6.cloned.1.call-start
  8.8 101.2 %all-gather.12.cloned.1.call-done = bf16[1,1024,1024]{2,1,0:T(8,128)(2,1)} async-done(((bf16[1,32,1024]{2,1,0:T(8,128)(2,1)}), bf16[1,1024,1024]{2,1,0:T(8,128)(2,1)}) %all-gather.12.cloned.1.call-update) | async-done | bytes 2097168 | tf_op jit(solution)/shard_map/all_gather | solution.py:15
  110.0 2.1 fusion.11
  112.1 0.3 stack.9
  112.4 0.0 copy-start.3
  112.4 59.8 %all_to_all.5 = bf16[32,32,1024]{2,1,0:T(8,128)(2,1)S(1)} all-to-all(bf16[32,32,1024]{2,1,0:T(8,128)(2,1)S(1)} %stack.9), channel_id=1, replica_groups=mesh['row'=32,'col'=16] {'row'}, dimensions={0} | all-to-all | bytes 4194304 | tf_op jit(solution)/shard_map/all_to_all | solution.py:18
  172.1 0.0 copy-start.2
  172.1 0.0 copy-done
  172.1 0.0 copy-done.3
  172.1 1.1 fusion.10
  173.2 0.0 all-gather.6.cloned.1.call-update
  173.3 0.0 all-gather.10.cloned.1.call-start
  173.3 0.7 all-gather.10.cloned.1.call-update
  174.0 0.0 all-gather.8.cloned.1.call-start
  174.1 89.1 %all-gather.6.cloned.1.call-done = bf16[1024,1024]{1,0:T(8,128)(2,1)} async-done(((bf16[32,1024]{1,0:T(8,128)(2,1)}), bf16[1024,1024]{1,0:T(8,128)(2,1)}) %all-gather.6.cloned.1.call-update) | async-done | bytes 2097168 | tf_op jit(solution)/shard_map/all_gather | solution.py:25
  263.2 0.0 copy-done.2
  263.2 2.7 convolution_convert_fusion
  265.9 0.0 all-gather.8.cloned.1.call-update
  265.9 0.0 copy-start.1
  265.9 4.0 copy.7
  269.9 0.0 copy-done.1
  269.9 0.7 pad_maximum_fusion
  270.5 97.3 %all-gather.10.cloned.1.call-done = bf16[1024,2048]{1,0:T(8,128)(2,1)} async-done(((bf16[1024,128]{1,0:T(8,128)(2,1)}), bf16[1024,2048]{1,0:T(8,128)(2,1)}) %all-gather.10.cloned.1.call-update) | async-done | bytes 4194320 | tf_op jit(solution)/shard_map/all_gather | solution.py:30
  367.8 99.6 %all-gather.8.cloned.1.call-done = bf16[1024,1024]{1,0:T(8,128)(2,1)} async-done(((bf16[32,1024]{1,0:T(8,128)(2,1)}), bf16[1024,1024]{1,0:T(8,128)(2,1)}) %all-gather.8.cloned.1.call-update) | async-done | bytes 2097168 | tf_op jit(solution)/shard_map/all_gather | solution.py:27
  467.4 9.4 %fusion.4 = bf16[1024,1024]{0,1:T(8,128)(2,1)} fusion(bf16[1024,1024]{0,1:T(8,128)(2,1)} %copy.7, bf16[1024,2048]{1,0:T(8,128)(2,1)} %all-gather.10.cloned.1.call-done, bf16[1024,1024]{1,0:T(8,128)(2,1)} %all-gather.8.cloned.1.call-done, bf16[1024,1024]{1,0:T(8,128)(2,1)S(1)} %bitcast.34), kind=kOutput, calls=%fused_computation.5 | convolution fusion | flops 4306501632 | bytes 12582912 | tf_op jit(solution)/shard_map/dot_general | solution.py:29
  476.8 3.9 copy.8
Async XLA Ops:
  7.2 165.0 %copy-start = (bf16[32,1024]{1,0:T(8,128)(2,1)S(1)}, bf16[32,1024]{1,0:T(8,128)(2,1)}, u32[]{:S(2)}) copy-start(bf16[32,1024]{1,0:T(8,128)(2,1)} %param.7) | copy-start | bytes 196612
  7.2 102.8 %all-gather.12.cloned.1.call-start = ((), (), s32[]{:S(2)}) async-start(), calls=%async_computation.4 | async-start | bytes 2162688 | tf_op jit(solution)/shard_map/all_gather | solution.py:15
  8.7 254.4 %all-gather.6.cloned.1.call-start = ((), (), s32[]{:S(2)}) async-start(), calls=%async_computation.1 | async-start | bytes 2162688 | tf_op jit(solution)/shard_map/all_gather | solution.py:25
  112.4 59.8 %copy-start.3 = (bf16[2,32,1024]{2,1,0:T(8,128)(2,1)S(1)}, bf16[2,32,1024]{2,1,0:T(8,128)(2,1)}, u32[]{:S(2)}) copy-start(bf16[2,32,1024]{2,1,0:T(8,128)(2,1)} %param.5) | copy-start | bytes 393220
  172.1 91.0 %copy-start.2 = (bf16[2,32,1024]{2,1,0:T(8,128)(2,1)S(1)}, bf16[2,32,1024]{2,1,0:T(8,128)(2,1)}, u32[]{:S(2)}) copy-start(bf16[2,32,1024]{2,1,0:T(8,128)(2,1)} %param.6) | copy-start | bytes 393220
  173.3 194.5 %all-gather.10.cloned.1.call-start = ((), (), s32[]{:S(2)}) async-start(), calls=%async_computation.3 | async-start | bytes 4456448 | tf_op jit(solution)/shard_map/all_gather | solution.py:30
  174.0 293.4 %all-gather.8.cloned.1.call-start = ((), (), s32[]{:S(2)}) async-start(), calls=%async_computation.2 | async-start | bytes 2162688 | tf_op jit(solution)/shard_map/all_gather | solution.py:27
  265.9 4.0 copy-start.1
Sparse Core Ops, SparseCore 0:
  12.0 97.9 all-gather.11
  173.4 89.7 all-gather.5
  265.2 102.5 all-gather.9
  371.0 96.3 all-gather.7
